TPU v7x, 32 devices: a whole 2x2x4 slice. The times are simulated.
32 devices in a mesh: section: 8 (over y, x, core), tensor: 4 (over z).
Axes of the slice: x: 2, y: 2, z: 4, core: 2. Of those that a mesh axis runs over, the one named last changes fastest.
Arguments:
- acts: bfloat16 [8, 2, 32, 4096], P('section', None, None, 'tensor'), may hold values from -6 to 6
- grads_in: bfloat16 [8, 2, 32, 4096], P('section', None, None, 'tensor'), may hold values from -6 to 6
- head_grads: bfloat16 [8, 2, 128, 512], P('section', None, None, 'tensor'), may hold values from -6 to 6
- types: int32 [8, 2, 32], P('section'), may hold values 0 or 1
- gains: bfloat16 [8, 2, 2, 1024], P('section'), may hold values from 0.3984375 to 1.59375
- w_query: bfloat16 [8, 2, 4096, 512], P('section', None, None, 'tensor'), may hold values from -0.09375 to 0.09375
- w_key: bfloat16 [8, 2, 4096, 128], P('section', None, None, 'tensor'), may hold values from -0.09375 to 0.09375
- w_value: bfloat16 [8, 2, 4096, 128], P('section', None, None, 'tensor'), may hold values from -0.09375 to 0.09375
Outputs:
- routed: bfloat16 [8, 2, 32, 4096], P('section', None, None, 'tensor')
All inputs are finite; a program needn't handle non-finite values. No bound on the sum of `types` on one device may be relied on, other than what follows from the above.
Results may differ from a plain program's by a relative error of at most 0.0055.
Values may be sent and summed in bfloat16 or wider, within the bound.
A program may use at most 64 MiB of HBM per device.

v0:
```python
import jax
import jax.numpy as jnp
from jax import lax
from jax.sharding import PartitionSpec as P

HEAD_DIM = 128
SUB = 4
epsilon = 1e-05


def swapped(value, axis, stride):
    mask = 2**stride
    pairs = [(source, source ^ mask) for source in range(lax.axis_size(axis))]
    return lax.ppermute(value, axis, pairs)


def shifted(value, axis, by):
    peers = lax.axis_size(axis)
    return lax.ppermute(value, axis, [(i, (i + by) % peers) for i in range(peers)])


def sum_columns(first, second):
    return (
        lax.psum_scatter(first, "tensor", scatter_dimension=2, tiled=True),
        lax.psum_scatter(second, "tensor", scatter_dimension=2, tiled=True),
    )


def collect_rows(member, position, levels, axis):
    for bit in range(levels):
        partner = swapped(member, "section", bit)
        upper_bit = position >> bit & 1
        member = jnp.where(
            upper_bit == 1,
            jnp.concatenate([partner, member], axis=axis),
            jnp.concatenate([member, partner], axis=axis),
        )
    return member


def halve_once(member, upper_bit, bit):
    half_rows = member.shape[1] // 2
    lower_rows = member[:, :half_rows]
    higher_rows = member[:, half_rows:]
    kept_rows = jnp.where(upper_bit == 1, higher_rows, lower_rows)
    sent_rows = jnp.where(upper_bit == 1, lower_rows, higher_rows)
    return kept_rows + swapped(sent_rows, "section", bit)


def reduce_rows(first, second, position, levels):
    for bit in reversed(range(levels)):
        upper_bit = position >> bit & 1
        first = halve_once(first, upper_bit, bit)
        second = halve_once(second, upper_bit, bit)
    return (first, second)


def per_device(acts, grads_in, head_grads, types, gains, w_query, w_key, w_value):
    tensors = lax.axis_size("tensor")
    section_count = lax.axis_size("section") // SUB
    levels = SUB.bit_length() - 1
    position = lax.axis_index("section") % SUB
    section_here = lax.axis_index("section") // SUB
    x_local = acts[0]
    grad_local = grads_in[0]
    out_grads = head_grads[0]
    w_query = w_query[0]
    w_key = w_key[0]
    w_value = w_value[0]
    x_cols = lax.all_gather(x_local, "tensor", axis=2, tiled=True)
    x_full = collect_rows(x_cols, position, levels, 1)
    kind_full = collect_rows(types[0].astype(jnp.bfloat16), position, levels, 1)
    gain_full = collect_rows(gains[0], position, levels, 2).astype(jnp.float32)
    tokens = x_full.shape[1]
    tokq = x_local.shape[1]
    width = x_full.shape[2]
    cols_dev = x_local.shape[2]
    x_float = x_full.astype(jnp.float32)
    inverse = lax.rsqrt(jnp.mean(x_float * x_float, axis=-1, keepdims=True) + epsilon)
    gain_rows = jnp.where(kind_full[..., None] > 0.5, gain_full[:, 1:2, :], gain_full[:, 0:1, :])
    normed = (x_float * inverse * gain_rows).astype(jnp.bfloat16)
    queries = jnp.einsum(
        "ctd,cdh->cth", normed, w_query, preferred_element_type=jnp.float32
    ).astype(jnp.bfloat16)
    key_part = jnp.einsum("ctd,cdh->cth", normed, w_key, preferred_element_type=jnp.float32).astype(
        jnp.bfloat16
    )
    value_part = jnp.einsum(
        "ctd,cdh->cth", normed, w_value, preferred_element_type=jnp.float32
    ).astype(jnp.bfloat16)
    key_rows, value_rows = (
        lax.all_gather(key_part, "tensor", axis=2, tiled=True),
        lax.all_gather(value_part, "tensor", axis=2, tiled=True),
    )
    softmax_scale = HEAD_DIM ** (-0.5)
    scores = (
        jnp.einsum("cqh,ckh->cqk", queries, key_rows, preferred_element_type=jnp.float32)
        * softmax_scale
    )
    causal = jnp.arange(tokens)[:, None] >= jnp.arange(tokens)[None, :]
    scores = jnp.where(causal[None], scores, -1e30)
    attn_probs = jax.nn.softmax(scores, axis=-1)
    probs_low = attn_probs.astype(jnp.bfloat16)
    prob_grads = jnp.einsum(
        "cqh,ckh->cqk", out_grads, value_rows, preferred_element_type=jnp.float32
    )
    score_grads = (
        attn_probs
        * (prob_grads - jnp.sum(prob_grads * attn_probs, axis=-1, keepdims=True))
        * softmax_scale
    ).astype(jnp.bfloat16)
    query_grads = jnp.einsum(
        "cqk,ckh->cqh", score_grads, key_rows, preferred_element_type=jnp.float32
    ).astype(jnp.bfloat16)
    key_each = jnp.einsum("cqk,cqh->ckh", score_grads, queries, preferred_element_type=jnp.float32)
    value_each = jnp.einsum(
        "cqk,cqh->ckh", probs_low, out_grads, preferred_element_type=jnp.float32
    )
    key_sum, value_sum = sum_columns(key_each, value_each)
    key_grads = key_sum.astype(jnp.bfloat16)
    value_grads = value_sum.astype(jnp.bfloat16)
    joined_grads = jnp.concatenate([query_grads, key_grads, value_grads], axis=2)
    joined_weights = jnp.concatenate([w_query, w_key, w_value], axis=2)
    partial_value = jnp.einsum(
        "cth,cdh->ctd", joined_grads, joined_weights, preferred_element_type=jnp.float32
    )
    stat_part = jnp.sum(x_float * gain_rows * partial_value, axis=-1)
    stat_wide = jnp.broadcast_to(stat_part[..., None], stat_part.shape + (tensors,))
    grad_rows_sum, stat_rows = reduce_rows(partial_value, stat_wide, position, levels)
    grad_mine, stat_mine = sum_columns(grad_rows_sum, stat_rows)
    my_inverse = lax.dynamic_slice_in_dim(inverse, position * tokq, tokq, 1)
    my_gain = lax.dynamic_slice_in_dim(gain_rows, position * tokq, tokq, 1)
    my_gain = lax.dynamic_slice_in_dim(my_gain, lax.axis_index("tensor") * cols_dev, cols_dev, 2)
    my_x = x_local.astype(jnp.float32)
    stat_mean = stat_mine / width
    norm_grads = my_inverse * my_gain * grad_mine - my_x * my_inverse**3 * stat_mean
    result = (grad_local.astype(jnp.float32) + norm_grads).astype(jnp.bfloat16)
    arrived = shifted(result, "section", -SUB)
    routed = jnp.where(section_here == section_count - 1, arrived[::-1], arrived)
    return routed[None]


def solution(mesh):
    return jax.shard_map(
        per_device,
        mesh=mesh,
        in_specs=(
            P("section", None, None, "tensor"),
            P("section", None, None, "tensor"),
            P("section", None, None, "tensor"),
            P("section", None, None),
            P("section", None, None, None),
            P("section", None, None, "tensor"),
            P("section", None, None, "tensor"),
            P("section", None, None, "tensor"),
        ),
        out_specs=P("section", None, None, "tensor"),
        check_vma=False,
    )
```

profile of v0, /device:TPU:0, one launch (start us, length us, event | category | flops | bytes accessed | tf_op | source)
XLA Modules:
  0.0 225.5 jit_solution(11091461946398277763)
XLA Ops:
  6.5 0.7 convert_bitcast_fusion
  7.3 0.5 collective-permute-start.2
  7.8 0.0 collective-permute-start.4
  7.8 17.7 %all-gather = bf16[1,2,32,4096]{3,2,1,0:T(8,128)(2,1)S(1)} all-gather(bf16[1,2,32,1024]{3,2,1,0:T(8,128)(2,1)} %param.8), channel_id=2, replica_groups=mesh['section'=8,'tensor'=4] {'tensor'}, dimensions={3}, use_global_device_ids=true | all-gather | bytes 655360 | tf_op jit(solution)/shard_map/all_gather | solution.py:70
  25.5 0.1 broadcast_select_fusion.6
  25.6 1.5 collective-permute-start.3
  27.1 0.8 broadcast_select_fusion.2
  27.9 0.6 collective-permute-start.5
  28.5 0.7 collective-permute-done.3
  29.2 0.1 fusion.52
  29.2 2.4 %collective-permute-done.5 = bf16[2,2,2048]{2,1,0:T(2,128)(2,1)S(1)} collective-permute-done((bf16[2,2,2048]{2,1,0:T(2,128)(2,1)S(1)}, bf16[2,2,2048]{2,1,0:T(2,128)(2,1)S(1)}, u32[]{:S(2)}, u32[]{:S(2)}) %collective-permute-start.5) | collective-permute-done | bytes 16416 | tf_op jit(solution)/shard_map/ppermute | solution.py:14
  31.7 0.2 maximum_select_fusion.1
  32.0 0.6 collective-permute-start.1
  32.6 0.1 fusion.60
  32.6 0.1 copy_bitcast_fusion
  32.7 23.5 %collective-permute-done.1 = bf16[2,64,4096]{2,1,0:T(8,128)(2,1)S(1)} collective-permute-done((bf16[2,64,4096]{2,1,0:T(8,128)(2,1)S(1)}, bf16[2,64,4096]{2,1,0:T(8,128)(2,1)S(1)}, u32[]{:S(2)}, u32[]{:S(2)}) %collective-permute-start.1) | collective-permute-done | bytes 1048608 | tf_op jit(solution)/shard_map/ppermute | solution.py:14
  56.2 0.8 fusion.2
  57.0 1.3 convolution_convert_fusion.2
  58.2 13.4 %all_gather.10 = bf16[2,128,128]{1,2,0:T(8,128)(2,1)S(1)} all-gather(bf16[2,128,32]{1,2,0:T(8,128)(2,1)S(1)} %convolution_convert_fusion.2), channel_id=1, replica_groups=mesh['section'=8,'tensor'=4] {'tensor'}, dimensions={2}, use_global_device_ids=true | all-gather | bytes 81920 | tf_op jit(solution)/shard_map/all_gather | solution.py:92
  71.7 1.3 convolution_convert_fusion.1
  72.9 13.2 %all_gather.11 = bf16[2,128,128]{1,2,0:T(8,128)(2,1)S(1)} all-gather(bf16[2,128,32]{1,2,0:T(8,128)(2,1)S(1)} %convolution_convert_fusion.1), channel_id=1, replica_groups=mesh['section'=8,'tensor'=4] {'tensor'}, dimensions={2}, use_global_device_ids=true | all-gather | bytes 81920 | tf_op jit(solution)/shard_map/all_gather | solution.py:93
  86.2 1.4 fusion.22
  87.5 0.2 fusion.18
  87.8 0.7 fusion.61
  88.5 0.9 fusion.43
  89.3 0.0 reduce-scatter.6.cloned.1.call-update
  89.4 0.0 reduce-scatter.4.cloned.1.call-start
  89.4 0.2 convolution_bitcast_fusion
  89.6 1.9 fusion.25
  91.5 0.0 reduce-scatter.4.cloned.1.call-update
  91.5 0.0 reduce-scatter.8.cloned.1.call-start
  91.6 2.8 %copy.11 = bf16[1,2,4096,128]{2,3,1,0:T(8,128)(2,1)} copy(bf16[1,2,4096,128]{3,2,1,0:T(8,128)(2,1)S(1)} %copy-done.1) | data formatting | bytes 4194304 | tf_op args[5]
  94.4 1.2 convolution_convert_fusion
  95.6 13.9 %reduce-scatter.6.cloned.1.call-done = f32[2,128,32]{1,2,0:T(8,128)} async-done(((f32[2,128,128]{1,2,0:T(8,128)}), f32[2,128,32]{1,2,0:T(8,128)}) %reduce-scatter.6.cloned.1.call-update) | async-done | bytes 32784 | tf_op jit(solution)/shard_map/reduce_scatter | solution.py:25
  109.5 0.8 convert_element_type.65
  110.2 19.1 %reduce-scatter.4.cloned.1.call-done = f32[2,128,32]{1,2,0:T(8,128)} async-done(((f32[2,128,128]{1,2,0:T(8,128)}), f32[2,128,32]{1,2,0:T(8,128)}) %reduce-scatter.4.cloned.1.call-update) | async-done | bytes 32784 | tf_op jit(solution)/shard_map/reduce_scatter | solution.py:24
  129.4 0.8 convert_element_type.63
  130.1 5.5 %fusion.6 = (f32[2,128]{1,0:T(2,128)S(1)}, f32[2,128,4096]{2,1,0:T(8,128)}, f32[2,128,4096]{2,1,0:T(8,128)S(1)}) fusion(f32[2,4096]{1,0:T(2,128)S(1)} %copy-done.6, f32[2,4096]{1,0:T(2,128)S(1)} %copy-done.8, pred[2,128]{1,0:T(4,128)(4,1)} %copy-done.11, bf16[2,64,4096]{2,1,0:T(8,128)(2,1)} %copy-done.2, bf16[2,64,4096]{2,1,0:T(8,128)(2,1)S(1)} %maximum_select_fusion.1, ...), kind=kOutput, calls=%fused_computation.9 | convolution fusion | flops 427065088 | bytes 13796609 | tf_op jit(solution)/shard_map/cth,cdh->ctd/dot_general | solution.py:124
  135.7 0.3 slice_select_fusion
  135.9 1.5 collective-permute-start.6
  137.5 43.5 %collective-permute-done.6 = f32[2,64,4096]{2,1,0:T(8,128)S(1)} collective-permute-done((f32[2,64,4096]{2,1,0:T(8,128)S(1)}, f32[2,64,4096]{2,1,0:T(8,128)S(1)}, u32[]{:S(2)}, u32[]{:S(2)}) %collective-permute-start.6) | collective-permute-done | bytes 2097184 | tf_op jit(solution)/shard_map/ppermute | solution.py:14
  181.0 0.4 select_add_fusion
  181.4 0.1 slice_select_fusion.1
  181.6 0.0 copy-start.14
  181.6 0.1 collective-permute-start.7
  181.7 2.6 %collective-permute-done.7 = f32[2,32,4096]{2,1,0:T(8,128)S(1)} collective-permute-done((f32[2,32,4096]{2,1,0:T(8,128)S(1)}, f32[2,32,4096]{2,1,0:T(8,128)S(1)}, u32[]{:S(2)}, u32[]{:S(2)}) %collective-permute-start.7) | collective-permute-done | bytes 1048608 | tf_op jit(solution)/shard_map/ppermute | solution.py:14
  184.3 1.2 select_add_fusion.1
  185.5 0.0 reduce-scatter.8.cloned.1.call-update
  185.6 0.1 broadcast_select_fusion.5
  185.6 1.5 collective-permute-start.8
  187.1 0.6 dynamic-slice.4
  187.7 1.6 collective-permute-done.8
  189.3 0.1 broadcast_select_fusion.3
  189.3 0.0 collective-permute-start.9
  189.4 0.1 fusion.50
  189.4 1.1 collective-permute-done.9
  190.5 0.1 select_add_fusion.2
  190.6 10.0 %all-reduce = f32[2,32,4]{1,0,2:T(2,128)S(1)} all-reduce(f32[2,32,4]{1,0,2:T(2,128)S(1)} %select_add_fusion.2), channel_id=6, replica_groups=mesh['section'=8,'tensor'=4] {'tensor'}, use_global_device_ids=true, to_apply=%region_8.9.clone | all-reduce | flops 256 | bytes 2048
  200.6 0.7 fusion.51
  201.2 10.7 %reduce-scatter.8.cloned.1.call-done = f32[2,32,1024]{2,1,0:T(8,128)} async-done(((f32[2,32,4096]{2,1,0:T(8,128)}), f32[2,32,1024]{2,1,0:T(8,128)}) %reduce-scatter.8.cloned.1.call-update) | async-done | bytes 262160 | tf_op jit(solution)/shard_map/reduce_scatter | solution.py:24
  212.0 1.2 fusion.32
  213.2 1.5 collective-permute-start.10
  214.8 3.5 %collective-permute-done.10 = bf16[2,32,1024]{2,1,0:T(8,128)(2,1)S(1)} collective-permute-done((bf16[2,32,1024]{2,1,0:T(8,128)(2,1)S(1)}, bf16[2,32,1024]{2,1,0:T(8,128)(2,1)S(1)}, u32[]{:S(2)}, u32[]{:S(2)}) %collective-permute-start.10) | collective-permute-done | bytes 131104 | tf_op jit(solution)/shard_map/ppermute | solution.py:19
  218.3 0.7 fusion.37
  (40 shorter events, 0.1 us)
Async XLA Ops:
  6.5 81.9 %copy-start = (bf16[1,2,128,128]{3,2,1,0:T(8,128)(2,1)S(1)}, bf16[1,2,128,128]{3,2,1,0:T(8,128)(2,1)}, u32[]{:S(2)}) copy-start(bf16[1,2,128,128]{3,2,1,0:T(8,128)(2,1)} %param.10) | copy-start | bytes 196612
  6.5 50.4 %copy-start.12 = (bf16[1,2,4096,32]{2,3,1,0:T(8,128)(2,1)S(1)}, bf16[1,2,4096,32]{2,3,1,0:T(8,128)(2,1)}, u32[]{:S(2)}) copy-start(bf16[1,2,4096,32]{2,3,1,0:T(8,128)(2,1)} %param.14) | copy-start | bytes 1572868
  6.5 102.9 %reduce-scatter.6.cloned.1.call-start = ((), (), s32[]{:S(2)}) async-start(), calls=%async_computation.4 | async-start | bytes 163840 | tf_op jit(solution)/shard_map/reduce_scatter | solution.py:25
  7.3 18.2 %collective-permute-start.2 = (bf16[2,32]{1,0:T(2,128)(2,1)S(1)}, bf16[2,32]{1,0:T(2,128)(2,1)S(1)}, u32[]{:S(2)}, u32[]{:S(2)}) collective-permute-start(bf16[2,32]{1,0:T(2,128)(2,1)S(1)} %convert_bitcast_fusion), channel_id=1, source_target_pairs={{0,4},{4,0},{8,12},{12,8},{16,20},{20,16},{24,28},{28,24},{1,5},{5... | collective-permute-start | bytes 392 | tf_op jit(solution)/shard_map/ppermute | solution.py:14
  7.8 19.3 %collective-permute-start.4 = (bf16[2,2,1024]{2,1,0:T(2,128)(2,1)}, bf16[2,2,1024]{2,1,0:T(2,128)(2,1)S(1)}, u32[]{:S(2)}, u32[]{:S(2)}) collective-permute-start(bf16[2,2,1024]{2,1,0:T(2,128)(2,1)} %bitcast.58), channel_id=1, source_target_pairs={{0,4},{4,0},{8,12},{12,8},{16,20},{20,16},{24,28},{28,24},{1,5},{5... | collective-permute-start | bytes 24584 | tf_op jit(solution)/shard_map/ppermute | solution.py:14
  25.5 6.3 %collective-permute-start = (bf16[2,32,4096]{2,1,0:T(8,128)(2,1)S(1)}, bf16[2,32,4096]{2,1,0:T(8,128)(2,1)S(1)}, u32[]{:S(2)}, u32[]{:S(2)}) collective-permute-start(bf16[2,32,4096]{2,1,0:T(8,128)(2,1)S(1)} %bitcast.52), channel_id=1, source_target_pairs={{0,4},{4,0},{8,12},{12,8},{16,20},{20,16},{24,28},{28,24},{1,5},{5... | collective-permute-start | bytes 1572872 | tf_op jit(solution)/shard_map/ppermute | solution.py:14
  25.6 3.6 %collective-permute-start.3 = (bf16[2,64]{1,0:T(2,128)(2,1)S(1)}, bf16[2,64]{1,0:T(2,128)(2,1)S(1)}, u32[]{:S(2)}, u32[]{:S(2)}) collective-permute-start(bf16[2,64]{1,0:T(2,128)(2,1)S(1)} %broadcast_select_fusion.6), channel_id=1, source_target_pairs={{0,8},{4,12},{8,0},{12,4},{16,24},{20,28},{24,16},{28,20},{1,9},{5... | collective-permute-start | bytes 776 | tf_op jit(solution)/shard_map/ppermute | solution.py:14
  27.9 3.8 %collective-permute-start.5 = (bf16[2,2,2048]{2,1,0:T(2,128)(2,1)S(1)}, bf16[2,2,2048]{2,1,0:T(2,128)(2,1)S(1)}, u32[]{:S(2)}, u32[]{:S(2)}) collective-permute-start(bf16[2,2,2048]{2,1,0:T(2,128)(2,1)S(1)} %broadcast_select_fusion.2), channel_id=1, source_target_pairs={{0,8},{4,12},{8,0},{12,4},{16,24},{20,28},{24,16},{28,20},{1,9},{5... | collective-permute-start | bytes 49160 | tf_op jit(solution)/shard_map/ppermute | solution.py:14
  29.2 56.9 %copy-start.11 = (pred[2,128]{1,0:T(4,128)(4,1)}, pred[2,128]{1,0:T(4,128)(4,1)S(1)}, u32[]{:S(2)}) copy-start(pred[2,128]{1,0:T(4,128)(4,1)S(1)} %fusion.52) | copy-start | bytes 772
  32.0 24.2 %collective-permute-start.1 = (bf16[2,64,4096]{2,1,0:T(8,128)(2,1)S(1)}, bf16[2,64,4096]{2,1,0:T(8,128)(2,1)S(1)}, u32[]{:S(2)}, u32[]{:S(2)}) collective-permute-start(bf16[2,64,4096]{2,1,0:T(8,128)(2,1)S(1)} %maximum_select_fusion.1), channel_id=1, source_target_pairs={{0,8},{4,12},{8,0},{12,4},{16,24},{20,28},{24,16},{28,20},{1,9},{5... | collective-permute-start | bytes 3145736 | tf_op jit(solution)/shard_map/ppermute | solution.py:14
  32.7 53.5 %copy-start.5 = (f32[2,4096]{1,0:T(2,128)}, f32[2,4096]{1,0:T(2,128)S(1)}, u32[]{:S(2)}) copy-start(f32[2,4096]{1,0:T(2,128)S(1)} %get-tuple-element.16) | copy-start | bytes 98308
  32.7 53.5 %copy-start.7 = (f32[2,4096]{1,0:T(2,128)}, f32[2,4096]{1,0:T(2,128)S(1)}, u32[]{:S(2)}) copy-start(f32[2,4096]{1,0:T(2,128)S(1)} %get-tuple-element.17) | copy-start | bytes 98308
  56.2 30.0 %copy-start.2 = (bf16[2,64,4096]{2,1,0:T(8,128)(2,1)}, bf16[2,64,4096]{2,1,0:T(8,128)(2,1)S(1)}, u32[]{:S(2)}) copy-start(bf16[2,64,4096]{2,1,0:T(8,128)(2,1)S(1)} %collective-permute-done.1) | copy-start | bytes 3145732
  56.9 29.2 %copy-start.9 = (f32[2,128]{1,0:T(2,128)}, f32[2,128]{1,0:T(2,128)S(1)}, u32[]{:S(2)}) copy-start(f32[2,128]{1,0:T(2,128)S(1)} %add_rsqrt_fusion) | copy-start | bytes 3076
  56.9 14.7 %copy-start.13 = (bf16[1,2,4096,32]{2,3,1,0:T(8,128)(2,1)S(1)}, bf16[1,2,4096,32]{2,3,1,0:T(8,128)(2,1)}, u32[]{:S(2)}) copy-start(bf16[1,2,4096,32]{2,3,1,0:T(8,128)(2,1)} %param.15) | copy-start | bytes 1572868
  71.7 14.5 %copy-start.1 = (bf16[1,2,4096,128]{3,2,1,0:T(8,128)(2,1)S(1)}, bf16[1,2,4096,128]{3,2,1,0:T(8,128)(2,1)}, u32[]{:S(2)}) copy-start(bf16[1,2,4096,128]{3,2,1,0:T(8,128)(2,1)} %param.13) | copy-start | bytes 6291460
  89.4 40.0 %reduce-scatter.4.cloned.1.call-start = ((), (), s32[]{:S(2)}) async-start(), calls=%async_computation.3 | async-start | bytes 163840 | tf_op jit(solution)/shard_map/reduce_scatter | solution.py:24
  89.6 40.5 %copy-start.6 = (f32[2,4096]{1,0:T(2,128)S(1)}, f32[2,4096]{1,0:T(2,128)}, u32[]{:S(2)}) copy-start(f32[2,4096]{1,0:T(2,128)} %copy-done.5) | copy-start | bytes 98308
  89.6 40.5 %copy-start.8 = (f32[2,4096]{1,0:T(2,128)S(1)}, f32[2,4096]{1,0:T(2,128)}, u32[]{:S(2)}) copy-start(f32[2,4096]{1,0:T(2,128)} %copy-done.7) | copy-start | bytes 98308
  91.5 120.5 %reduce-scatter.8.cloned.1.call-start = ((), (), s32[]{:S(2)}) async-start(), calls=%async_computation.5 | async-start | bytes 1310720 | tf_op jit(solution)/shard_map/reduce_scatter | solution.py:24
  135.9 45.1 %collective-permute-start.6 = (f32[2,64,4096]{2,1,0:T(8,128)S(1)}, f32[2,64,4096]{2,1,0:T(8,128)S(1)}, u32[]{:S(2)}, u32[]{:S(2)}) collective-permute-start(f32[2,64,4096]{2,1,0:T(8,128)S(1)} %slice_select_fusion), channel_id=1, source_target_pairs={{0,8},{4,12},{8,0},{12,4},{16,24},{20,28},{24,16},{28,20},{1,9},{5... | collective-permute-start | bytes 6291464 | tf_op jit(solution)/shard_map/ppermute | solution.py:14
  181.6 5.5 %copy-start.14 = (u32[32]{0:T(128)S(1)}, u32[32]{0:T(128)}, u32[]{:S(2)}) copy-start(u32[32]{0:T(128)} %constant.90) | copy-start | bytes 388
  181.6 7.8 %copy-start.10 = (f32[2,128]{1,0:T(2,128)S(1)}, f32[2,128]{1,0:T(2,128)}, u32[]{:S(2)}) copy-start(f32[2,128]{1,0:T(2,128)} %copy-done.9) | copy-start | bytes 3076
  181.6 30.4 %copy-start.3 = (bf16[1,2,32,1024]{3,2,1,0:T(8,128)(2,1)S(1)}, bf16[1,2,32,1024]{3,2,1,0:T(8,128)(2,1)}, u32[]{:S(2)}) copy-start(bf16[1,2,32,1024]{3,2,1,0:T(8,128)(2,1)} %param.8) | copy-start | bytes 393220
  181.6 30.4 %copy-start.4 = (bf16[1,2,32,1024]{3,2,1,0:T(8,128)(2,1)S(1)}, bf16[1,2,32,1024]{3,2,1,0:T(8,128)(2,1)}, u32[]{:S(2)}) copy-start(bf16[1,2,32,1024]{3,2,1,0:T(8,128)(2,1)} %param.9) | copy-start | bytes 393220
  181.6 2.7 %collective-permute-start.7 = (f32[2,32,4096]{2,1,0:T(8,128)S(1)}, f32[2,32,4096]{2,1,0:T(8,128)S(1)}, u32[]{:S(2)}, u32[]{:S(2)}) collective-permute-start(f32[2,32,4096]{2,1,0:T(8,128)S(1)} %slice_select_fusion.1), channel_id=1, source_target_pairs={{0,4},{4,0},{8,12},{12,8},{16,20},{20,16},{24,28},{28,24},{1,5},{5... | collective-permute-start | bytes 3145736 | tf_op jit(solution)/shard_map/ppermute | solution.py:14
  185.6 3.6 %collective-permute-start.8 = (f32[2,64,4]{1,0,2:T(2,128)S(1)}, f32[2,64,4]{1,0,2:T(2,128)S(1)}, u32[]{:S(2)}, u32[]{:S(2)}) collective-permute-start(f32[2,64,4]{1,0,2:T(2,128)S(1)} %broadcast_in_dim.67), channel_id=1, source_target_pairs={{0,8},{4,12},{8,0},{12,4},{16,24},{20,28},{24,16},{28,20},{1,9},{5... | collective-permute-start | bytes 6152 | tf_op jit(solution)/shard_map/ppermute | solution.py:14
  189.3 1.2 collective-permute-start.9
  213.2 5.0 %collective-permute-start.10 = (bf16[2,32,1024]{2,1,0:T(8,128)(2,1)S(1)}, bf16[2,32,1024]{2,1,0:T(8,128)(2,1)S(1)}, u32[]{:S(2)}, u32[]{:S(2)}) collective-permute-start(bf16[2,32,1024]{2,1,0:T(8,128)(2,1)S(1)} %fusion.32), channel_id=1, source_target_pairs={{0,16},{4,20},{8,24},{12,28},{16,0},{20,4},{24,8},{28,12},{1,17},{... | collective-permute-start | bytes 393224 | tf_op jit(solution)/shard_map/ppermute | solution.py:19
Sparse Core Ops, SparseCore 0:
  89.5 19.9 reduce-scatter.5
  111.7 17.5 reduce-scatter.3
  185.7 26.2 reduce-scatter.7
where the time goes:
time: 226 us; the launch traced here: 225 us
  waiting for transfers between devices  123 us (54%)
  blocking collectives  54.3 us (24%)
  matrix products  13.8 us (6%)
  between operations  13.4 us (6%)
  other arithmetic  9.83 us (4%)
  starting transfers between devices  7.91 us (4%)
  local copies, waits for them, and re-layouts  3.58 us (2%)
    ppermute x10, waiting for transfers between devices, swapped(): return lax.ppermute(value, axis, pairs)  75.4 us
    reduce_scatter x2, waiting for transfers between devices, sum_columns(): lax.psum_scatter(first, 'tensor', scatter_dimension=2, tiled=True)  29.9 us
    all_gather x1, blocking collectives, per_device(): x_cols = lax.all_gather(x_local, 'tensor', axis=2, tiled=True)  17.7 us
    reduce_scatter x1, waiting for transfers between devices, sum_columns(): lax.psum_scatter(second, 'tensor', scatter_dimension=2, tiled=True)  13.9 us
    all_gather x1, blocking collectives, per_device(): lax.all_gather(key_part, 'tensor', axis=2, tiled=True)  13.4 us
    all_gather x1, blocking collectives, per_device(): lax.all_gather(value_part, 'tensor', axis=2, tiled=True)  13.2 us
    unnamed x1, blocking collectives  10 us
    ppermute x10, starting transfers between devices, swapped(): return lax.ppermute(value, axis, pairs)  6.29 us
  transfers between devices with their start and end apart: 14, of which 11 were waited for; matrix products, arithmetic and copies ran while one was open for 4% of the time, Pallas kernels for 0%

commit v1 on v0

--- a/solution.py
+++ b/solution.py
@@ -6,6 +6,27 @@
 HEAD_DIM = 128
 SUB = 4
 epsilon = 1e-05
+
+
+def collect(value, axis, dim):
+    devices, place, rows = (lax.axis_size(axis), lax.axis_index(axis), value.shape[dim])
+    upward = [(i, (i + 1) % devices) for i in range(devices)]
+    behind = [(i, (i - 1) % devices) for i in range(devices)]
+    whole = jnp.zeros((*value.shape[:dim], devices * rows, *value.shape[dim + 1 :]), value.dtype)
+    whole = lax.dynamic_update_slice_in_dim(whole, value, place * rows, axis=dim)
+    from_left = from_right = value
+    halfway = devices // 2
+    for turn in range(1, halfway + 1):
+        from_left = lax.ppermute(from_left, axis, upward)
+        whole = lax.dynamic_update_slice_in_dim(
+            whole, from_left, (place - turn) % devices * rows, axis=dim
+        )
+        if turn < devices - halfway:
+            from_right = lax.ppermute(from_right, axis, behind)
+            whole = lax.dynamic_update_slice_in_dim(
+                whole, from_right, (place + turn) % devices * rows, axis=dim
+            )
+    return whole
 
 
 def swapped(value, axis, stride):
@@ -67,7 +88,7 @@
     w_query = w_query[0]
     w_key = w_key[0]
     w_value = w_value[0]
-    x_cols = lax.all_gather(x_local, "tensor", axis=2, tiled=True)
+    x_cols = collect(x_local, "tensor", 2)
     x_full = collect_rows(x_cols, position, levels, 1)
     kind_full = collect_rows(types[0].astype(jnp.bfloat16), position, levels, 1)
     gain_full = collect_rows(gains[0], position, levels, 2).astype(jnp.float32)

time: 226 us -> 219 us (0.969)
  blocking collectives: 54.3 us -> 36.3 us
  starting transfers between devices: 7.91 us -> 14.2 us
  waiting for transfers between devices: 123 us -> 126 us
    all_gather x1 -> x0, blocking collectives: 17.7 us -> none  [per_device(): x_cols = lax.all_gather(x_local, 'tensor', axis=2, tiled=True)]
    ppermute x0 -> x3, waiting for transfers between devices: none -> 6.8 us  [the longest x2 6.12 us: collect(): from_left = lax.ppermute(from_left, axis, upward)]
    ppermute x0 -> x3, starting transfers between devices: none -> 5.08 us  [the longest x2 3.05 us: collect(): from_left = lax.ppermute(from_left, axis, upward)]
  transfers between devices with their start and end apart: 14 -> 17, of which waited for: 11 -> 12; matrix products, arithmetic and copies ran while one was open for 4% -> 5% of each run, Pallas kernels for 0% -> 0%
where the time goes in v1:
time: 219 us; the launch traced here: 218 us
  waiting for transfers between devices  126 us (58%)
  blocking collectives  36.3 us (17%)
  starting transfers between devices  14.2 us (6%)
  matrix products  13.7 us (6%)
  between operations  13.4 us (6%)
  other arithmetic  9.78 us (4%)
  local copies, waits for them, and re-layouts  4.61 us (2%)
    ppermute x10, waiting for transfers between devices, swapped(): return lax.ppermute(value, axis, pairs)  74 us
    reduce_scatter x2, waiting for transfers between devices, sum_columns(): lax.psum_scatter(first, 'tensor', scatter_dimension=2, tiled=True)  29.9 us
    all_gather x1, blocking collectives, per_device(): lax.all_gather(key_part, 'tensor', axis=2, tiled=True)  13.1 us
    all_gather x1, blocking collectives, per_device(): lax.all_gather(value_part, 'tensor', axis=2, tiled=True)  13.1 us
    reduce_scatter x1, waiting for transfers between devices, sum_columns(): lax.psum_scatter(second, 'tensor', scatter_dimension=2, tiled=True)  12.3 us
    unnamed x1, blocking collectives  10 us
    ppermute x10, starting transfers between devices, swapped(): return lax.ppermute(value, axis, pairs)  7.45 us
    ppermute x2, waiting for transfers between devices, collect(): from_left = lax.ppermute(from_left, axis, upward)  6.12 us
  transfers between devices with their start and end apart: 17, of which 12 were waited for; matrix products, arithmetic and copies ran while one was open for 5% of the time, Pallas kernels for 0%

profile of v1, /device:TPU:0, one launch (start us, length us, event | category | flops | bytes accessed | tf_op | source)
XLA Modules:
  0.0 218.4 jit_solution(9109123076796079554)
XLA Ops:
  6.5 3.1 %collective-permute-start = (bf16[2,32,1024]{2,1,0:T(8,128)(2,1)}, bf16[2,32,1024]{2,1,0:T(8,128)(2,1)S(1)}, u32[]{:S(2)}, u32[]{:S(2)}) collective-permute-start(bf16[2,32,1024]{2,1,0:T(8,128)(2,1)} %bitcast.52), channel_id=1, source_target_pairs={{0,1},{1,2},{2,3},{3,0},{4,5},{5,6},{6,7},{7,4},{8,9},{9,10},{10,1... | collective-permute-start | bytes 393224 | tf_op jit(solution)/shard_map/ppermute | solution.py:20
  9.6 2.0 collective-permute-start.1
  11.6 0.7 convert_bitcast_fusion
  12.3 0.5 collective-permute-start.7
  12.9 1.0 constant_dynamic-update-slice_fusion.3
  13.9 0.1 broadcast_select_fusion.6
  14.0 1.7 collective-permute-start.6
  15.7 0.8 broadcast_select_fusion.2
  16.5 0.4 collective-permute-start.8
  16.9 0.7 collective-permute-done.1
  17.6 6.1 %collective-permute-done.2 = bf16[2,32,1024]{2,1,0:T(8,128)(2,1)S(1)} collective-permute-done((bf16[2,32,1024]{2,1,0:T(8,128)(2,1)S(1)}, bf16[2,32,1024]{2,1,0:T(8,128)(2,1)S(1)}, u32[]{:S(2)}, u32[]{:S(2)}) %collective-permute-start.2) | collective-permute-done | bytes 131104 | tf_op jit(solution)/shard_map/ppermute | solution.py:20
  23.7 0.1 collective-permute-start.3
  23.8 0.1 fusion.49
  23.9 1.8 collective-permute-done.3
  25.7 0.2 maximum_select_fusion.1
  25.9 1.7 collective-permute-start.4
  27.6 0.1 fusion.57
  27.7 0.1 copy_bitcast_fusion
  27.7 23.4 %collective-permute-done.4 = bf16[2,64,4096]{2,1,0:T(8,128)(2,1)S(1)} collective-permute-done((bf16[2,64,4096]{2,1,0:T(8,128)(2,1)S(1)}, bf16[2,64,4096]{2,1,0:T(8,128)(2,1)S(1)}, u32[]{:S(2)}, u32[]{:S(2)}) %collective-permute-start.4) | collective-permute-done | bytes 1048608 | tf_op jit(solution)/shard_map/ppermute | solution.py:35
  51.2 0.8 fusion.2
  52.0 1.3 convolution_convert_fusion.2
  53.2 13.1 %all_gather.6 = bf16[2,128,128]{1,2,0:T(8,128)(2,1)S(1)} all-gather(bf16[2,128,32]{1,2,0:T(8,128)(2,1)S(1)} %convolution_convert_fusion.2), channel_id=1, replica_groups=mesh['section'=8,'tensor'=4] {'tensor'}, dimensions={2}, use_global_device_ids=true | all-gather | bytes 81920 | tf_op jit(solution)/shard_map/all_gather | solution.py:113
  66.4 1.3 convolution_convert_fusion.1
  67.7 13.1 %all_gather.7 = bf16[2,128,128]{1,2,0:T(8,128)(2,1)S(1)} all-gather(bf16[2,128,32]{1,2,0:T(8,128)(2,1)S(1)} %convolution_convert_fusion.1), channel_id=1, replica_groups=mesh['section'=8,'tensor'=4] {'tensor'}, dimensions={2}, use_global_device_ids=true | all-gather | bytes 81920 | tf_op jit(solution)/shard_map/all_gather | solution.py:114
  80.8 1.4 fusion.22
  82.2 0.2 fusion.18
  82.4 0.7 fusion.58
  83.1 0.9 fusion.40
  84.0 0.0 reduce-scatter.6.cloned.1.call-update
  84.0 0.0 reduce-scatter.4.cloned.1.call-start
  84.1 0.2 convolution_bitcast_fusion
  84.3 1.9 fusion.25
  86.2 0.0 reduce-scatter.8.cloned.1.call-start
  86.2 2.8 %copy.11 = bf16[1,2,4096,128]{2,3,1,0:T(8,128)(2,1)} copy(bf16[1,2,4096,128]{3,2,1,0:T(8,128)(2,1)S(1)} %copy-done.1) | data formatting | bytes 4194304 | tf_op args[5]
  89.0 1.2 convolution_convert_fusion
  90.2 12.3 %reduce-scatter.6.cloned.1.call-done = f32[2,128,32]{1,2,0:T(8,128)} async-done(((f32[2,128,128]{1,2,0:T(8,128)}), f32[2,128,32]{1,2,0:T(8,128)}) %reduce-scatter.6.cloned.1.call-update) | async-done | bytes 32784 | tf_op jit(solution)/shard_map/reduce_scatter | solution.py:46
  102.5 0.8 convert_element_type.65
  103.2 19.1 %reduce-scatter.4.cloned.1.call-done = f32[2,128,32]{1,2,0:T(8,128)} async-done(((f32[2,128,128]{1,2,0:T(8,128)}), f32[2,128,32]{1,2,0:T(8,128)}) %reduce-scatter.4.cloned.1.call-update) | async-done | bytes 32784 | tf_op jit(solution)/shard_map/reduce_scatter | solution.py:45
  122.3 0.8 convert_element_type.63
  123.1 5.5 %fusion.6 = (f32[2,128]{1,0:T(2,128)S(1)}, f32[2,128,4096]{2,1,0:T(8,128)}, f32[2,128,4096]{2,1,0:T(8,128)S(1)}) fusion(f32[2,4096]{1,0:T(2,128)S(1)} %copy-done.6, f32[2,4096]{1,0:T(2,128)S(1)} %copy-done.8, pred[2,128]{1,0:T(4,128)(4,1)} %copy-done.11, bf16[2,64,4096]{2,1,0:T(8,128)(2,1)} %copy-done.2, bf16[2,64,4096]{2,1,0:T(8,128)(2,1)S(1)} %maximum_select_fusion.1, ...), kind=kOutput, calls=%fused_computation.9 | convolution fusion | flops 427065088 | bytes 13796609 | tf_op jit(solution)/shard_map/cth,cdh->ctd/dot_general | solution.py:145
  128.6 0.3 slice_select_fusion
  128.9 1.5 collective-permute-start.9
  130.4 43.5 %collective-permute-done.9 = f32[2,64,4096]{2,1,0:T(8,128)S(1)} collective-permute-done((f32[2,64,4096]{2,1,0:T(8,128)S(1)}, f32[2,64,4096]{2,1,0:T(8,128)S(1)}, u32[]{:S(2)}, u32[]{:S(2)}) %collective-permute-start.9) | collective-permute-done | bytes 2097184 | tf_op jit(solution)/shard_map/ppermute | solution.py:35
  173.9 0.4 select_add_fusion
  174.4 0.1 slice_select_fusion.1
  174.5 0.1 collective-permute-start.10
  174.6 2.6 %collective-permute-done.10 = f32[2,32,4096]{2,1,0:T(8,128)S(1)} collective-permute-done((f32[2,32,4096]{2,1,0:T(8,128)S(1)}, f32[2,32,4096]{2,1,0:T(8,128)S(1)}, u32[]{:S(2)}, u32[]{:S(2)}) %collective-permute-start.10) | collective-permute-done | bytes 1048608 | tf_op jit(solution)/shard_map/ppermute | solution.py:35
  177.3 1.2 select_add_fusion.1
  178.4 0.0 reduce-scatter.8.cloned.1.call-update
  178.5 0.1 broadcast_select_fusion.5
  178.6 1.5 collective-permute-start.11
  180.0 0.6 dynamic-slice.4
  180.6 1.6 collective-permute-done.11
  182.2 0.1 broadcast_select_fusion.3
  182.3 0.1 fusion.47
  182.4 1.1 collective-permute-done.12
  183.4 0.1 select_add_fusion.2
  183.5 10.0 %all-reduce = f32[2,32,4]{1,0,2:T(2,128)S(1)} all-reduce(f32[2,32,4]{1,0,2:T(2,128)S(1)} %select_add_fusion.2), channel_id=5, replica_groups=mesh['section'=8,'tensor'=4] {'tensor'}, use_global_device_ids=true, to_apply=%region_8.9.clone | all-reduce | flops 256 | bytes 2048
  193.5 0.7 fusion.48
  194.2 10.8 %reduce-scatter.8.cloned.1.call-done = f32[2,32,1024]{2,1,0:T(8,128)} async-done(((f32[2,32,4096]{2,1,0:T(8,128)}), f32[2,32,1024]{2,1,0:T(8,128)}) %reduce-scatter.8.cloned.1.call-update) | async-done | bytes 262160 | tf_op jit(solution)/shard_map/reduce_scatter | solution.py:45
  204.9 1.2 fusion.29
  206.2 1.6 collective-permute-start.13
  207.8 3.4 %collective-permute-done.13 = bf16[2,32,1024]{2,1,0:T(8,128)(2,1)S(1)} collective-permute-done((bf16[2,32,1024]{2,1,0:T(8,128)(2,1)S(1)}, bf16[2,32,1024]{2,1,0:T(8,128)(2,1)S(1)}, u32[]{:S(2)}, u32[]{:S(2)}) %collective-permute-start.13) | collective-permute-done | bytes 131104 | tf_op jit(solution)/shard_map/ppermute | solution.py:40
  211.2 0.7 fusion.34
  (50 shorter events, 0.3 us)
Async XLA Ops:
  6.5 76.6 %copy-start = (bf16[1,2,128,128]{3,2,1,0:T(8,128)(2,1)S(1)}, bf16[1,2,128,128]{3,2,1,0:T(8,128)(2,1)}, u32[]{:S(2)}) copy-start(bf16[1,2,128,128]{3,2,1,0:T(8,128)(2,1)} %param.10) | copy-start | bytes 196612
  6.5 95.9 %reduce-scatter.6.cloned.1.call-start = ((), (), s32[]{:S(2)}) async-start(), calls=%async_computation.4 | async-start | bytes 163840 | tf_op jit(solution)/shard_map/reduce_scatter | solution.py:46
  6.5 10.3 %collective-permute-start = (bf16[2,32,1024]{2,1,0:T(8,128)(2,1)}, bf16[2,32,1024]{2,1,0:T(8,128)(2,1)S(1)}, u32[]{:S(2)}, u32[]{:S(2)}) collective-permute-start(bf16[2,32,1024]{2,1,0:T(8,128)(2,1)} %bitcast.52), channel_id=1, source_target_pairs={{0,1},{1,2},{2,3},{3,0},{4,5},{5,6},{6,7},{7,4},{8,9},{9,10},{10,1... | collective-permute-start | bytes 393224 | tf_op jit(solution)/shard_map/ppermute | solution.py:20
  9.6 8.0 %collective-permute-start.1 = (bf16[2,32,1024]{2,1,0:T(8,128)(2,1)}, bf16[2,32,1024]{2,1,0:T(8,128)(2,1)S(1)}, u32[]{:S(2)}, u32[]{:S(2)}) collective-permute-start(bf16[2,32,1024]{2,1,0:T(8,128)(2,1)} %bitcast.53), channel_id=1, source_target_pairs={{0,3},{1,0},{2,1},{3,2},{4,7},{5,4},{6,5},{7,6},{8,11},{9,8},{10,9... | collective-permute-start | bytes 393224 | tf_op jit(solution)/shard_map/ppermute | solution.py:25
  12.3 1.6 collective-permute-start.5
  12.3 3.4 %collective-permute-start.7 = (bf16[2,2,1024]{2,1,0:T(2,128)(2,1)}, bf16[2,2,1024]{2,1,0:T(2,128)(2,1)S(1)}, u32[]{:S(2)}, u32[]{:S(2)}) collective-permute-start(bf16[2,2,1024]{2,1,0:T(2,128)(2,1)} %bitcast.57), channel_id=1, source_target_pairs={{0,4},{4,0},{8,12},{12,8},{16,20},{20,16},{24,28},{28,24},{1,5},{5... | collective-permute-start | bytes 24584 | tf_op jit(solution)/shard_map/ppermute | solution.py:35
  12.8 39.1 %copy-start.12 = (bf16[1,2,4096,32]{2,3,1,0:T(8,128)(2,1)S(1)}, bf16[1,2,4096,32]{2,3,1,0:T(8,128)(2,1)}, u32[]{:S(2)}) copy-start(bf16[1,2,4096,32]{2,3,1,0:T(8,128)(2,1)} %param.14) | copy-start | bytes 1572868
  14.0 9.8 %collective-permute-start.6 = (bf16[2,64]{1,0:T(2,128)(2,1)S(1)}, bf16[2,64]{1,0:T(2,128)(2,1)S(1)}, u32[]{:S(2)}, u32[]{:S(2)}) collective-permute-start(bf16[2,64]{1,0:T(2,128)(2,1)S(1)} %broadcast_select_fusion.6), channel_id=1, source_target_pairs={{0,8},{4,12},{8,0},{12,4},{16,24},{20,28},{24,16},{28,20},{1,9},{5... | collective-permute-start | bytes 776 | tf_op jit(solution)/shard_map/ppermute | solution.py:35
  16.5 7.4 %collective-permute-start.8 = (bf16[2,2,2048]{2,1,0:T(2,128)(2,1)S(1)}, bf16[2,2,2048]{2,1,0:T(2,128)(2,1)S(1)}, u32[]{:S(2)}, u32[]{:S(2)}) collective-permute-start(bf16[2,2,2048]{2,1,0:T(2,128)(2,1)S(1)} %broadcast_select_fusion.2), channel_id=1, source_target_pairs={{0,8},{4,12},{8,0},{12,4},{16,24},{20,28},{24,16},{28,20},{1,9},{5... | collective-permute-start | bytes 49160 | tf_op jit(solution)/shard_map/ppermute | solution.py:35
  16.9 6.8 %collective-permute-start.2 = (bf16[2,32,1024]{2,1,0:T(8,128)(2,1)S(1)}, bf16[2,32,1024]{2,1,0:T(8,128)(2,1)S(1)}, u32[]{:S(2)}, u32[]{:S(2)}) collective-permute-start(bf16[2,32,1024]{2,1,0:T(8,128)(2,1)S(1)} %collective-permute-done), channel_id=1, source_target_pairs={{0,1},{1,2},{2,3},{3,0},{4,5},{5,6},{6,7},{7,4},{8,9},{9,10},{10,1... | collective-permute-start | bytes 393224 | tf_op jit(solution)/shard_map/ppermute | solution.py:20
  23.7 2.0 collective-permute-start.3
  23.9 56.9 %copy-start.11 = (pred[2,128]{1,0:T(4,128)(4,1)}, pred[2,128]{1,0:T(4,128)(4,1)S(1)}, u32[]{:S(2)}) copy-start(pred[2,128]{1,0:T(4,128)(4,1)S(1)} %fusion.49) | copy-start | bytes 772
  25.9 25.3 %collective-permute-start.4 = (bf16[2,64,4096]{2,1,0:T(8,128)(2,1)S(1)}, bf16[2,64,4096]{2,1,0:T(8,128)(2,1)S(1)}, u32[]{:S(2)}, u32[]{:S(2)}) collective-permute-start(bf16[2,64,4096]{2,1,0:T(8,128)(2,1)S(1)} %maximum_select_fusion.1), channel_id=1, source_target_pairs={{0,8},{4,12},{8,0},{12,4},{16,24},{20,28},{24,16},{28,20},{1,9},{5... | collective-permute-start | bytes 3145736 | tf_op jit(solution)/shard_map/ppermute | solution.py:35
  27.7 53.1 %copy-start.5 = (f32[2,4096]{1,0:T(2,128)}, f32[2,4096]{1,0:T(2,128)S(1)}, u32[]{:S(2)}) copy-start(f32[2,4096]{1,0:T(2,128)S(1)} %get-tuple-element.16) | copy-start | bytes 98308
  27.7 53.0 %copy-start.7 = (f32[2,4096]{1,0:T(2,128)}, f32[2,4096]{1,0:T(2,128)S(1)}, u32[]{:S(2)}) copy-start(f32[2,4096]{1,0:T(2,128)S(1)} %get-tuple-element.17) | copy-start | bytes 98308
  51.2 29.6 %copy-start.2 = (bf16[2,64,4096]{2,1,0:T(8,128)(2,1)}, bf16[2,64,4096]{2,1,0:T(8,128)(2,1)S(1)}, u32[]{:S(2)}) copy-start(bf16[2,64,4096]{2,1,0:T(8,128)(2,1)S(1)} %collective-permute-done.4) | copy-start | bytes 3145732
  51.9 28.9 %copy-start.9 = (f32[2,128]{1,0:T(2,128)}, f32[2,128]{1,0:T(2,128)S(1)}, u32[]{:S(2)}) copy-start(f32[2,128]{1,0:T(2,128)S(1)} %add_rsqrt_fusion) | copy-start | bytes 3076
  52.0 14.4 %copy-start.13 = (bf16[1,2,4096,32]{2,3,1,0:T(8,128)(2,1)S(1)}, bf16[1,2,4096,32]{2,3,1,0:T(8,128)(2,1)}, u32[]{:S(2)}) copy-start(bf16[1,2,4096,32]{2,3,1,0:T(8,128)(2,1)} %param.15) | copy-start | bytes 1572868
  66.4 14.4 %copy-start.1 = (bf16[1,2,4096,128]{3,2,1,0:T(8,128)(2,1)S(1)}, bf16[1,2,4096,128]{3,2,1,0:T(8,128)(2,1)}, u32[]{:S(2)}) copy-start(bf16[1,2,4096,128]{3,2,1,0:T(8,128)(2,1)} %param.13) | copy-start | bytes 6291460
  84.0 38.3 %reduce-scatter.4.cloned.1.call-start = ((), (), s32[]{:S(2)}) async-start(), calls=%async_computation.3 | async-start | bytes 163840 | tf_op jit(solution)/shard_map/reduce_scatter | solution.py:45
  84.3 38.8 %copy-start.6 = (f32[2,4096]{1,0:T(2,128)S(1)}, f32[2,4096]{1,0:T(2,128)}, u32[]{:S(2)}) copy-start(f32[2,4096]{1,0:T(2,128)} %copy-done.5) | copy-start | bytes 98308
  84.3 38.8 %copy-start.8 = (f32[2,4096]{1,0:T(2,128)S(1)}, f32[2,4096]{1,0:T(2,128)}, u32[]{:S(2)}) copy-start(f32[2,4096]{1,0:T(2,128)} %copy-done.7) | copy-start | bytes 98308
  86.2 118.8 %reduce-scatter.8.cloned.1.call-start = ((), (), s32[]{:S(2)}) async-start(), calls=%async_computation.5 | async-start | bytes 1310720 | tf_op jit(solution)/shard_map/reduce_scatter | solution.py:45
  128.9 45.0 %collective-permute-start.9 = (f32[2,64,4096]{2,1,0:T(8,128)S(1)}, f32[2,64,4096]{2,1,0:T(8,128)S(1)}, u32[]{:S(2)}, u32[]{:S(2)}) collective-permute-start(f32[2,64,4096]{2,1,0:T(8,128)S(1)} %slice_select_fusion), channel_id=1, source_target_pairs={{0,8},{4,12},{8,0},{12,4},{16,24},{20,28},{24,16},{28,20},{1,9},{5... | collective-permute-start | bytes 6291464 | tf_op jit(solution)/shard_map/ppermute | solution.py:35
  174.5 5.6 %copy-start.14 = (u32[32]{0:T(128)S(1)}, u32[32]{0:T(128)}, u32[]{:S(2)}) copy-start(u32[32]{0:T(128)} %constant.108) | copy-start | bytes 388
  174.5 7.8 %copy-start.10 = (f32[2,128]{1,0:T(2,128)S(1)}, f32[2,128]{1,0:T(2,128)}, u32[]{:S(2)}) copy-start(f32[2,128]{1,0:T(2,128)} %copy-done.9) | copy-start | bytes 3076
  174.5 30.4 %copy-start.3 = (bf16[1,2,32,1024]{3,2,1,0:T(8,128)(2,1)S(1)}, bf16[1,2,32,1024]{3,2,1,0:T(8,128)(2,1)}, u32[]{:S(2)}) copy-start(bf16[1,2,32,1024]{3,2,1,0:T(8,128)(2,1)} %param.8) | copy-start | bytes 393220
  174.5 30.4 %copy-start.4 = (bf16[1,2,32,1024]{3,2,1,0:T(8,128)(2,1)S(1)}, bf16[1,2,32,1024]{3,2,1,0:T(8,128)(2,1)}, u32[]{:S(2)}) copy-start(bf16[1,2,32,1024]{3,2,1,0:T(8,128)(2,1)} %param.9) | copy-start | bytes 393220
  174.5 2.7 %collective-permute-start.10 = (f32[2,32,4096]{2,1,0:T(8,128)S(1)}, f32[2,32,4096]{2,1,0:T(8,128)S(1)}, u32[]{:S(2)}, u32[]{:S(2)}) collective-permute-start(f32[2,32,4096]{2,1,0:T(8,128)S(1)} %slice_select_fusion.1), channel_id=1, source_target_pairs={{0,4},{4,0},{8,12},{12,8},{16,20},{20,16},{24,28},{28,24},{1,5},{5... | collective-permute-start | bytes 3145736 | tf_op jit(solution)/shard_map/ppermute | solution.py:35
  178.6 3.6 %collective-permute-start.11 = (f32[2,64,4]{1,0,2:T(2,128)S(1)}, f32[2,64,4]{1,0,2:T(2,128)S(1)}, u32[]{:S(2)}, u32[]{:S(2)}) collective-permute-start(f32[2,64,4]{1,0,2:T(2,128)S(1)} %broadcast_in_dim.71), channel_id=1, source_target_pairs={{0,8},{4,12},{8,0},{12,4},{16,24},{20,28},{24,16},{28,20},{1,9},{5... | collective-permute-start | bytes 6152 | tf_op jit(solution)/shard_map/ppermute | solution.py:35
  182.3 1.2 collective-permute-start.12
  206.2 5.0 %collective-permute-start.13 = (bf16[2,32,1024]{2,1,0:T(8,128)(2,1)S(1)}, bf16[2,32,1024]{2,1,0:T(8,128)(2,1)S(1)}, u32[]{:S(2)}, u32[]{:S(2)}) collective-permute-start(bf16[2,32,1024]{2,1,0:T(8,128)(2,1)S(1)} %fusion.29), channel_id=1, source_target_pairs={{0,16},{4,20},{8,24},{12,28},{16,0},{20,4},{24,8},{28,12},{1,17},{... | collective-permute-start | bytes 393224 | tf_op jit(solution)/shard_map/ppermute | solution.py:40
Sparse Core Ops, SparseCore 0:
  84.1 18.2 reduce-scatter.5
  104.7 17.5 reduce-scatter.3
  178.6 26.2 reduce-scatter.7
